TPU v7x, 256 devices: a whole 4x4x8 slice. The times are simulated.
256 devices in a mesh: row: 32 (over z_lo, y, core), col: 8 (over x, z_hi).
Axes of the slice: x: 4, y: 4, z: 8 (z_hi: 2, z_lo: 4; z = z_hi * 4 + z_lo), core: 2. Of those that a mesh axis runs over, the one named last changes fastest.
Arguments:
- stem_slab: float32 [2, 256, 256, 1024], P(None, 'row', None, 'col'), may hold values from -6 to 6
- factors: float32 [256, 2, 2, 256, 256], P(('row', 'col')), may hold values from -0.25 to 0.25
- branch_owner: int32 [4], replicated, may hold values from 0 to 255
- entangle_phase: float32 [4, 256, 256], replicated, may hold values from -3.140625 to 3.140625
Outputs:
- contracted: float32 [2, 256, 256, 1024], P(None, 'row', None, 'col')
All inputs are finite; a program needn't handle non-finite values.
Results may differ from a plain program's by a relative error of at most 0.000039.
Values sent between devices are 32-bit elements; how exact they have to be, the bound alone decides.
A program may use at most 64 MiB of HBM per device.

v0:
```python
from functools import partial

import jax
import jax.numpy as jnp
from jax import lax
from jax.sharding import PartitionSpec as P

STEPS = 4


def from_root(array, axis, root):
    mine = lax.axis_index(axis) == root
    return lax.psum(jnp.where(mine, array, jnp.zeros_like(array)), axis)


def complex_mix(stacked, branch, form):
    mix = partial(jnp.einsum, form, precision=lax.Precision.HIGHEST)
    real_part, imag_part = (stacked[0], stacked[1])
    branch_real, branch_imag = (branch[0], branch[1])
    return jnp.stack(
        [
            mix(real_part, branch_real) - mix(imag_part, branch_imag),
            mix(real_part, branch_imag) + mix(imag_part, branch_real),
        ]
    )


def rotate(stacked, angles):
    cosine = jnp.cos(angles)[:, :, None]
    sine = jnp.sin(angles)[:, :, None]
    real_part, imag_part = (stacked[0], stacked[1])
    return jnp.stack([real_part * cosine - imag_part * sine, real_part * sine + imag_part * cosine])


def build_branch(owned):
    dot_high = partial(jnp.dot, precision=lax.Precision.HIGHEST)
    left_real, left_imag = (owned[0, 0], owned[0, 1])
    right_real, right_imag = (owned[1, 0], owned[1, 1])
    return jnp.stack(
        [
            dot_high(left_real, right_real) - dot_high(left_imag, right_imag),
            dot_high(left_real, right_imag) + dot_high(left_imag, right_real),
        ]
    )


def first_group(stem_local, branch, angles_all, row_index):
    pieces = lax.all_to_all(stem_local, "row", split_axis=2, concat_axis=1, tiled=True)
    pieces = complex_mix(pieces, branch, "akb,al->lkb")
    width_part = pieces.shape[2]
    angles = lax.dynamic_slice_in_dim(angles_all, row_index * width_part, width_part, 1)
    pieces = rotate(pieces, angles)
    return lax.all_to_all(pieces, "row", split_axis=1, concat_axis=2, tiled=True)


def on_device(stem_slab, factors, branch_owner, entangle_phase):
    own_branch = build_branch(factors[0])
    row_index = lax.axis_index("row")
    branches = []
    for step in range(STEPS):
        branches.append(from_root(own_branch, ("row", "col"), branch_owner[step]))
    rows_local = stem_slab.shape[1]
    stem_local = stem_slab
    for step in range(STEPS):
        if step % 2 == 0:
            stem_local = complex_mix(stem_local, branches[step], "akb,kl->alb")
            angles = lax.dynamic_slice_in_dim(
                entangle_phase[step], row_index * rows_local, rows_local, 0
            )
            stem_local = rotate(stem_local, angles)
        else:
            stem_local = first_group(stem_local, branches[step], entangle_phase[step], row_index)
    return stem_local


def solution(mesh):
    return jax.shard_map(
        on_device,
        mesh=mesh,
        in_specs=(P(None, "row", None, "col"), P(("row", "col"), None, None, None, None), P(), P()),
        out_specs=P(None, "row", None, "col"),
        check_vma=False,
    )
```

profile of v0, /device:TPU:1, one launch (start us, length us, event | category | flops | bytes accessed | tf_op | source)
XLA Modules:
  0.0 545.1 jit_solution(10839674288626867920)
XLA Ops:
  6.5 1.5 fusion.22
  8.0 1.4 fusion.23
  9.5 1.5 fusion.25
  13.5 1.4 fusion.4
  15.0 0.4 fusion.5
  15.4 1.4 broadcast_select_fusion.3
  16.7 0.4 copy-done.6
  17.2 0.9 fusion.24
  18.1 263.4 %all-reduce.3.cloned.1.call-done = (f32[2,256,256]{2,1,0:T(8,128)}, f32[2,256,256]{2,1,0:T(8,128)}, f32[2,256,256]{2,1,0:T(8,128)}, f32[2,256,256]{2,1,0:T(8,128)}) async-done(((f32[2,256,256]{2,1,0:T(8,128)}, f32[2,256,256]{2,1,0:T(8,128)}, f32[2,256,256]{2,1,0:T(8,128)}, f32[2,256,256]{2,1,0:T(8,128)}), (f32[2,256,256]{2,1,0:T(8,128)}, f32[2,256,256]{2,1,0:T(8,128)}, f32[2,256,256]{2,1,0:T(8,128)}, ...) | async-done | bytes 2097168 | tf_op jit(solution)/shard_map/psum | solution.py:13
  281.5 2.0 fusion.8
  283.6 1.1 fusion.10
  284.7 1.1 fusion.2
  285.8 1.6 subtract_bitcast_fusion.3
  287.4 0.2 pad_maximum_fusion
  287.6 2.5 copy.36
  290.1 9.8 %all-to-all-start = ((f32[2,8,256,128]{3,1,0,2:T(8,128)}), f32[2,8,256,128]{3,1,0,2:T(8,128)S(1)}, u32[]{:S(2)}, u32[]{:S(2)}) async-start(f32[2,8,256,128]{3,1,0,2:T(8,128)} %copy.36), calls=%async_computation | async-start | bytes 4194304 | tf_op jit(solution)/shard_map/all_to_all | solution.py:48
  300.0 1.1 cosine_bitcast_fusion
  301.2 46.9 %all-to-all-done = f32[2,8,256,128]{3,1,0,2:T(8,128)S(1)} async-done(((f32[2,8,256,128]{3,1,0,2:T(8,128)}), f32[2,8,256,128]{3,1,0,2:T(8,128)S(1)}, u32[]{:S(2)}, u32[]{:S(2)}) %all-to-all-start) | async-done | bytes 2097184 | tf_op jit(solution)/shard_map/all_to_all | solution.py:48
  348.1 0.2 copy.99
  348.3 0.8 copy-done.4
  349.1 1.0 fusion.12
  350.2 1.0 fusion.13
  351.2 1.1 convolution_add_fusion.2
  352.3 1.6 subtract_bitcast_fusion.2
  353.9 0.2 pad_maximum_fusion.1
  354.1 2.5 copy.44
  356.7 6.4 %all-to-all-start.1 = ((f32[2,256,8,128]{3,2,0,1:T(8,128)}), f32[2,256,8,128]{3,2,0,1:T(8,128)S(1)}, u32[]{:S(2)}, u32[]{:S(2)}) async-start(f32[2,256,8,128]{3,2,0,1:T(8,128)} %copy.44), calls=%async_computation.1 | async-start | bytes 4194304 | tf_op jit(solution)/shard_map/all_to_all | solution.py:53
  363.0 0.8 cosine_bitcast_fusion.2
  363.8 47.4 %all-to-all-done.1 = f32[2,256,8,128]{3,2,0,1:T(8,128)S(1)} async-done(((f32[2,256,8,128]{3,2,0,1:T(8,128)}), f32[2,256,8,128]{3,2,0,1:T(8,128)S(1)}, u32[]{:S(2)}, u32[]{:S(2)}) %all-to-all-start.1) | async-done | bytes 2097184 | tf_op jit(solution)/shard_map/all_to_all | solution.py:53
  411.2 0.2 copy.98
  411.4 0.8 copy-done.3
  412.2 1.0 fusion.14
  413.3 1.0 fusion.15
  414.3 1.1 fusion
  415.4 1.6 subtract_bitcast_fusion.1
  417.0 0.2 pad_maximum_fusion.2
  417.2 2.5 copy.50
  419.7 6.4 %all-to-all-start.2 = ((f32[2,8,256,128]{3,1,0,2:T(8,128)}), f32[2,8,256,128]{3,1,0,2:T(8,128)S(1)}, u32[]{:S(2)}, u32[]{:S(2)}) async-start(f32[2,8,256,128]{3,1,0,2:T(8,128)} %copy.50), calls=%async_computation.2 | async-start | bytes 4194304 | tf_op jit(solution)/shard_map/all_to_all | solution.py:48
  426.2 48.0 %all-to-all-done.2 = f32[2,8,256,128]{3,1,0,2:T(8,128)S(1)} async-done(((f32[2,8,256,128]{3,1,0,2:T(8,128)}), f32[2,8,256,128]{3,1,0,2:T(8,128)S(1)}, u32[]{:S(2)}, u32[]{:S(2)}) %all-to-all-start.2) | async-done | bytes 2097184 | tf_op jit(solution)/shard_map/all_to_all | solution.py:48
  474.2 0.2 copy.97
  474.4 0.8 copy-done.2
  475.3 1.0 fusion.16
  476.3 1.0 fusion.17
  477.4 1.1 convolution_add_fusion
  478.5 1.6 subtract_bitcast_fusion
  480.3 1.2 copy.58
  481.5 55.2 %all_to_all.63 = f32[2,256,8,128]{3,2,0,1:T(8,128)S(1)} all-to-all(f32[2,256,8,128]{3,2,0,1:T(8,128)S(1)} %copy.58), channel_id=1, replica_groups=mesh['row'=32,'col'=8] {'row'}, dimensions={1} | all-to-all | bytes 4194304 | tf_op jit(solution)/shard_map/all_to_all | solution.py:53
  536.7 1.5 copy.96
  (20 shorter events, 0.5 us)
Async XLA Ops:
  6.5 8.4 %copy-start.1 = (f32[1,2,2,256,256]{4,3,2,1,0:T(8,128)S(1)}, f32[1,2,2,256,256]{4,3,2,1,0:T(8,128)}, u32[]{:S(2)}) copy-start(f32[1,2,2,256,256]{4,3,2,1,0:T(8,128)} %param.5) | copy-start | bytes 3145732
  6.5 275.0 %all-reduce.3.cloned.1.call-start = ((), (), s32[]{:S(2)}) async-start(), calls=%async_computation.4 | async-start | bytes 4194304 | tf_op jit(solution)/shard_map/psum | solution.py:13
  15.3 1.8 copy-start.6
  16.7 264.8 %copy-start = (f32[2,8,256,128]{3,2,1,0:T(8,128)S(1)}, f32[2,8,256,128]{3,2,1,0:T(8,128)}, u32[]{:S(2)}) copy-start(f32[2,8,256,128]{3,2,1,0:T(8,128)} %param.4) | copy-start | bytes 6291460
  281.5 2.1 copy-start.5
  290.1 9.8 %copy-start.7 = (f32[1,256,256]{2,1,0:T(8,128)S(1)}, f32[1,256,256]{2,1,0:T(8,128)}, u32[]{:S(2)}) copy-start(f32[1,256,256]{2,1,0:T(8,128)} %get-tuple-element.18) | copy-start | bytes 786436
  290.1 58.0 %all-to-all-start = ((f32[2,8,256,128]{3,1,0,2:T(8,128)}), f32[2,8,256,128]{3,1,0,2:T(8,128)S(1)}, u32[]{:S(2)}, u32[]{:S(2)}) async-start(f32[2,8,256,128]{3,1,0,2:T(8,128)} %copy.36), calls=%async_computation | async-start | bytes 4194304 | tf_op jit(solution)/shard_map/all_to_all | solution.py:48
  348.1 1.0 copy-start.4
  356.7 54.5 %all-to-all-start.1 = ((f32[2,256,8,128]{3,2,0,1:T(8,128)}), f32[2,256,8,128]{3,2,0,1:T(8,128)S(1)}, u32[]{:S(2)}, u32[]{:S(2)}) async-start(f32[2,256,8,128]{3,2,0,1:T(8,128)} %copy.44), calls=%async_computation.1 | async-start | bytes 4194304 | tf_op jit(solution)/shard_map/all_to_all | solution.py:53
  411.2 1.0 copy-start.3
  419.7 54.5 %all-to-all-start.2 = ((f32[2,8,256,128]{3,1,0,2:T(8,128)}), f32[2,8,256,128]{3,1,0,2:T(8,128)S(1)}, u32[]{:S(2)}, u32[]{:S(2)}) async-start(f32[2,8,256,128]{3,1,0,2:T(8,128)} %copy.50), calls=%async_computation.2 | async-start | bytes 4194304 | tf_op jit(solution)/shard_map/all_to_all | solution.py:48
  474.2 1.0 copy-start.2
Sparse Core Ops, SparseCore 0:
  16.9 264.6 all-reduce.2
where the time goes:
time: 546 us; the launch traced here: 545 us
  waiting for transfers between devices  406 us (74%)
  blocking collectives  55.2 us (10%)
  matrix products  24.8 us (5%)
  starting transfers between devices  22.5 us (4%)
  local copies, waits for them, and re-layouts  18.4 us (3%)
  between operations  16.3 us (3%)
    psum x1, waiting for transfers between devices, from_root(): return lax.psum(jnp.where(mine, array, jnp.zeros_like(array)), axis)  263 us
    all_to_all x2, waiting for transfers between devices, first_group(): lax.all_to_all(stem_local, 'row', split_axis=2, concat_axis=1, tiled=True)  94.9 us
    all_to_all x1, blocking collectives, first_group(): lax.all_to_all(pieces, 'row', split_axis=1, concat_axis=2, tiled=True)  55.2 us
    all_to_all x1, waiting for transfers between devices, first_group(): lax.all_to_all(pieces, 'row', split_axis=1, concat_axis=2, tiled=True)  47.4 us
    all_to_all x2, starting transfers between devices, first_group(): lax.all_to_all(stem_local, 'row', split_axis=2, concat_axis=1, tiled=True)  16.2 us
  transfers between devices with their start and end apart: 4, of which 4 were waited for; matrix products, arithmetic and copies ran while one was open for 1% of the time, Pallas kernels for 0%

commit v1 on v0

v1 whole, which is shorter than its diff:
```python
import functools

import jax
import jax.numpy as jnp
from jax import lax
from jax.experimental import pallas as pl
from jax.experimental.pallas import tpu as pltpu
from jax.sharding import PartitionSpec as P

MESH = pl.DeviceIdType.MESH
F32 = jnp.float32
BF16 = jnp.bfloat16
STEPS = 4

NX, NY, NZ, NC = 4, 4, 8, 2
N_ROW = 32
BATCHES = ((1, 8), (8, 16), (16, 17), (17, 18), (18, 19), (19, 32))


def split(value):
    high = value.astype(BF16)
    return high, (value - high.astype(F32)).astype(BF16)


def dot3(left, right):
    (lh, ll), (rh, rl) = left, right
    dot = functools.partial(jnp.dot, preferred_element_type=F32)
    return dot(lh, rh) + (dot(lh, rl) + dot(ll, rh))


def drained(ref, sem):
    pltpu.make_async_copy(ref, ref, sem).wait()


def kernel(
    owner, factors, stem, phase, out,
    recv, mixed, cosine, sine, own, raw0, raw1, slots, from_y, summed, from_z, full,
    high, low, send, land, a_send, a_land, b_send, b_land, local,
):
    row, col = lax.axis_index("row"), lax.axis_index("col")
    core, y, z_lo = row % 2, (row // 2) % 4, row // 8
    x, z_hi = col // 2, col % 2
    z = z_hi * 4 + z_lo

    def at_core(c):
        return (z_lo * 8 + y * 2 + c, col)

    def at_x(i):
        return (row, i * 2 + z_hi)

    def at_y(i):
        return (z_lo * 8 + i * 2 + core, col)

    def at_z(i):
        return ((i % 4) * 8 + y * 2 + core, x * 2 + i // 4)

    def row_peer(i):
        peer = ((z_lo + i % 4) % 4) * 8 + (row + i // 4) % 8
        return peer

    barrier = pltpu.get_barrier_semaphore()

    def greet(device):
        pl.semaphore_signal(barrier, inc=1, device_id=device, device_id_type=MESH)

    @pl.loop(1, N_ROW)
    def _(i):
        greet((row_peer(i), col))

    @pl.loop(1, NX)
    def _(i):
        greet(at_x((x + i) % NX))

    @pl.loop(0, NZ // 2)
    def _(i):
        greet(at_z((1 - z_hi) * 4 + i))

    dot = functools.partial(jnp.dot, precision=lax.Precision.HIGHEST, preferred_element_type=F32)
    own[0] = dot(factors[0, 0], factors[1, 0]) - dot(factors[0, 1], factors[1, 1])
    own[1] = dot(factors[0, 0], factors[1, 1]) + dot(factors[0, 1], factors[1, 0])

    pl.semaphore_wait(barrier, N_ROW - 1 + NX - 1 + NZ // 2)

    def push(src, dst, stage, device):
        pltpu.make_async_remote_copy(
            src_ref=src, dst_ref=dst, send_sem=send.at[stage], recv_sem=land.at[stage],
            device_id=device, device_id_type=MESH,
        ).start()

    def stem_batch(first, last):
        @pl.loop(first, last)
        def _(i):
            peer = row_peer(i)
            pltpu.make_async_remote_copy(
                src_ref=stem.at[:, pl.ds(peer * 4, 4)],
                dst_ref=recv.at[:, :, pl.ds(row * 8, 8)],
                send_sem=a_send, recv_sem=a_land,
                device_id=(peer, col), device_id_type=MESH,
            ).start()

    push(own.at[1 - core], raw0.at[core], 0, at_core(1 - core))
    keep = pltpu.make_async_copy(
        stem.at[:, pl.ds(row * 4, 4)], recv.at[:, :, pl.ds(row * 8, 8)], local.at[0]
    )
    keep.start()
    stem_batch(*BATCHES[0])
    raw0[core] = own[core]
    drained(raw0.at[0], land.at[0])

    @pl.loop(1, NX)
    def _(i):
        peer = (x + i) % NX
        push(raw0.at[:, pl.ds(peer * 64, 64)], raw1.at[x], 1, at_x(peer))

    stem_batch(*BATCHES[1])
    raw1[x] = raw0[:, pl.ds(x * 64, 64)]

    @pl.loop(0, STEPS)
    def _(step):
        @pl.loop(0, 32)
        def _(i):
            angle = phase[step, pl.ds(i * 8, 8)]
            cosine[step, pl.ds(i * 8, 8)] = jnp.cos(angle)
            sine[step, pl.ds(i * 8, 8)] = jnp.sin(angle)

    drained(raw1.at[pl.ds(0, NX - 1)], land.at[1])
    for step in range(STEPS):
        at = owner[step]
        at_row, at_col = lax.shift_right_logical(at, 3), at & 7
        at_z_y = (at_col & 1) * 4 + lax.shift_right_logical(at_row, 3), lax.shift_right_logical(at_row, 1) & 3
        here = jnp.logical_and(at_z_y[0] == z, at_z_y[1] == y)
        value = raw1[lax.shift_right_logical(at_col, 1), at_row & 1]
        slots[step] = jnp.where(here, value, jnp.zeros_like(value))

    @pl.loop(1, NY)
    def _(i):
        peer = (y + i) % NY
        push(slots.at[:, pl.ds(peer * 16, 16)], from_y.at[y], 2, at_y(peer))

    stem_batch(*BATCHES[2])
    from_y[y] = slots[:, pl.ds(y * 16, 16)]
    drained(from_y.at[pl.ds(0, NY - 1)], land.at[2])
    total = (from_y[0] + from_y[1]) + (from_y[2] + from_y[3])
    summed[...] = total.reshape(NZ, 8, 256)

    @pl.loop(1, NZ)
    def _(i):
        peer = (z + i) % NZ
        push(summed.at[peer], from_z.at[z], 3, at_z(peer))

    stem_batch(*BATCHES[3])
    from_z[z] = summed[z]
    drained(from_z.at[pl.ds(0, NZ - 1)], land.at[3])
    total = from_z[0]
    for i in range(1, NZ):
        total = total + from_z[i]
    mine = full.at[:, core, x, y]
    eighth = full.at[z // 2, core, x, y, z % 2]
    eighth[...] = total

    @pl.loop(1, NZ)
    def _(i):
        push(eighth, eighth, 4, at_z((z + i) % NZ))

    stem_batch(*BATCHES[4])
    drained(from_z.at[pl.ds(0, NZ - 1)], land.at[4])

    @pl.loop(1, NY)
    def _(i):
        push(mine, mine, 5, at_y((y + i) % NY))

    drained(from_y.at[pl.ds(0, NY - 1)], land.at[5])
    quarter = full.at[:, core, x]

    @pl.loop(1, NX)
    def _(i):
        push(quarter, quarter, 6, at_x((x + i) % NX))

    stem_batch(*BATCHES[5])
    drained(full.at[pl.ds(0, NX - 1), 0], land.at[6])
    half = full.at[:, core]
    push(half, half, 7, at_core(1 - core))
    drained(half, land.at[7])

    for step in range(STEPS):
        for part in range(2):
            branch = full[step, part].reshape(256, 256)
            if step % 2:
                branch = branch.T
            high[step, part], low[step, part] = split(branch)

    keep.wait()
    drained(stem.at[:, pl.ds(0, (N_ROW - 1) * 4)], a_land)

    @pl.loop(0, 4)
    def _(b):
        real, imag = recv[0, b], recv[1, b]
        for step in range(STEPS):
            xr, xi = split(real), split(imag)
            br = (high[step, 0], low[step, 0])
            bi = (high[step, 1], low[step, 1])
            if step % 2:
                yr = dot3(br, xr) - dot3(bi, xi)
                yi = dot3(bi, xr) + dot3(br, xi)
            else:
                yr = dot3(xr, br) - dot3(xi, bi)
                yi = dot3(xr, bi) + dot3(xi, br)
            real = yr * cosine[step] - yi * sine[step]
            imag = yr * sine[step] + yi * cosine[step]
        mixed[b, 0] = real
        mixed[b, 1] = imag
        pltpu.make_async_copy(
            mixed.at[b, :, pl.ds(row * 8, 8)], out.at[:, row * 4 + b], local.at[1]
        ).start()

        @pl.loop(1, N_ROW)
        def _(i):
            peer = row_peer(i)
            pltpu.make_async_remote_copy(
                src_ref=mixed.at[b, :, pl.ds(peer * 8, 8)],
                dst_ref=out.at[:, row * 4 + b],
                send_sem=b_send, recv_sem=b_land,
                device_id=(peer, col), device_id_type=MESH,
            ).start()

    drained(out.at[:, pl.ds(0, 4)], local.at[1])
    drained(out.at[:, pl.ds(0, (N_ROW - 1) * 4)], b_land)
    drained(raw0.at[0], send.at[0])
    drained(raw1.at[pl.ds(0, NX - 1)], send.at[1])
    drained(from_y.at[pl.ds(0, NY - 1)], send.at[2])
    drained(from_z.at[pl.ds(0, NZ - 1)], send.at[3])
    drained(from_z.at[pl.ds(0, NZ - 1)], send.at[4])
    drained(from_y.at[pl.ds(0, NY - 1)], send.at[5])
    drained(full.at[pl.ds(0, NX - 1), 0], send.at[6])
    drained(full.at[:, 0], send.at[7])
    drained(stem.at[:, pl.ds(0, (N_ROW - 1) * 4)], a_send)
    drained(out.at[:, pl.ds(0, (N_ROW - 1) * 4)], b_send)


def on_device(stem_slab, factors, branch_owner, entangle_phase):
    stem = stem_slab.transpose(0, 3, 1, 2)
    vmem, dma = pltpu.VMEM, pltpu.SemaphoreType.DMA
    out = pl.pallas_call(
        kernel,
        out_shape=jax.ShapeDtypeStruct((2, 128, 8, 256), F32),
        in_specs=[
            pl.BlockSpec(memory_space=pltpu.SMEM),
            pl.BlockSpec(memory_space=pltpu.VMEM),
            pl.BlockSpec(memory_space=pl.ANY),
            pl.BlockSpec(memory_space=pltpu.VMEM),
        ],
        out_specs=pl.BlockSpec(memory_space=pl.ANY),
        scratch_shapes=[
            vmem((2, 4, 256, 256), F32),
            vmem((4, 2, 256, 256), F32),
            vmem((4, 256, 256), F32),
            vmem((4, 256, 256), F32),
            vmem((2, 256, 256), F32),
            vmem((2, 256, 256), F32),
            vmem((4, 2, 64, 256), F32),
            vmem((4, 64, 256), F32),
            vmem((4, 4, 16, 256), F32),
            vmem((8, 8, 256), F32),
            vmem((8, 8, 256), F32),
            vmem((4, 2, 4, 4, 2, 8, 256), F32),
            vmem((4, 2, 256, 256), BF16),
            vmem((4, 2, 256, 256), BF16),
            dma((8,)), dma((8,)),
            dma(()), dma(()), dma(()), dma(()),
            dma((2,)),
        ],
        compiler_params=pltpu.CompilerParams(collective_id=0, has_side_effects=True),
    )(branch_owner, factors[0], stem, entangle_phase)
    return out.transpose(0, 2, 3, 1)


def solution(mesh):
    return jax.shard_map(
        on_device,
        mesh=mesh,
        in_specs=(P(None, "row", None, "col"), P(("row", "col"), None, None, None, None), P(), P()),
        out_specs=P(None, "row", None, "col"),
        check_vma=False,
    )
```

time: 546 us -> 123 us (0.23)
  waiting for transfers between devices: 406 us -> 0 us
  Pallas kernels: 0 us -> 117 us
  blocking collectives: 55.2 us -> 0 us
  matrix products: 24.8 us -> 0 us
  starting transfers between devices: 22.5 us -> 0 us
  between operations: 16.3 us -> 0.01 us
  local copies, waits for them, and re-layouts: 18.4 us -> 5.97 us
    psum x1 -> x0, waiting for transfers between devices: 263 us -> none  [from_root(): return lax.psum(jnp.where(mine, array, jnp.zeros_like(array)), axis)]
    all_to_all x3 -> x0, waiting for transfers between devices: 142 us -> none  [the longest x2 94.9 us: first_group(): lax.all_to_all(stem_local, 'row', split_axis=2, concat_axis=1, tiled=True)]
    pallas_call x0 -> x1, Pallas kernels: none -> 117 us  [on_device(): pl.pallas_call(kernel, out_shape=jax.ShapeDtypeStruct((2, 128, 8, 256), F...]
    all_to_all x1 -> x0, blocking collectives: 55.2 us -> none  [first_group(): lax.all_to_all(pieces, 'row', split_axis=1, concat_axis=2, tiled=True)]
    dot_general x20 -> x0, matrix products: 24.8 us -> none  [the longest x4 6.34 us: complex_mix(): mix(imag_part, branch_imag)]
    all_to_all x3 -> x0, starting transfers between devices: 22.5 us -> none  [the longest x2 16.2 us: first_group(): lax.all_to_all(stem_local, 'row', split_axis=2, concat_axis=1, tiled=True)]
    another operation x4 -> x0, local copies, waits for them, and re-layouts: 8.83 us -> none  [rotate(): jnp.stack([real_part * cosine - imag_part * sine, real_part * sine + imag...]
  transfers between devices with their start and end apart: 4 -> 0, of which waited for: 4 -> 0; matrix products, arithmetic and copies ran while one was open for 1% -> 0% of each run, Pallas kernels for 0% -> 0%
where the time goes in v1:
time: 123 us
  Pallas kernels  117 us (95%)
  local copies, waits for them, and re-layouts  5.97 us (5%)
    pallas_call x1, Pallas kernels, on_device(): pl.pallas_call(kernel, out_shape=jax.ShapeDtypeStruct((2, 128, 8, 256), F...  117 us
    unnamed x1, local copies, waits for them, and re-layouts  3.03 us
    transpose x1, local copies, waits for them, and re-layouts, on_device(): return out.transpose(0, 2, 3, 1)  2.94 us

profile of v1, /device:TPU:1, one launch (start us, length us, event | category | flops | bytes accessed | tf_op | source)
XLA Modules:
  0.0 123.0 jit_solution(1438616582176824275)
XLA Ops:
  0.0 3.0 %copy.5 = f32[2,8,256,128]{2,1,3,0:T(8,128)} copy(f32[2,8,256,128]{3,2,1,0:T(8,128)} %param.4) | data formatting | bytes 4194304 | tf_op args[0]
  3.0 117.0 %shard_map.46 = f32[2,128,8,256]{3,2,1,0:T(8,128)} custom-call(s32[4]{0:T(128)} %owner.1, f32[2,2,256,256]{3,2,1,0:T(8,128)} %bitcast.5, f32[2,128,8,256]{3,2,1,0:T(8,128)} %bitcast.4, f32[4,256,256]{2,1,0:T(8,128)} %phase.1), custom_call_target="tpu_custom_call" | custom-call | tf_op jit(solution)/shard_map/pallas_call | solution.py:243
  120.0 2.9 %copy.6 = f32[2,8,256,128]{3,2,1,0:T(8,128)} copy(f32[2,8,256,128]{2,1,3,0:T(8,128)} %bitcast.3) | data formatting | bytes 4194304 | tf_op jit(solution)/shard_map/transpose | solution.py:274

commit v2 on v1

--- a/solution.py
+++ b/solution.py
@@ -14,7 +14,8 @@
 
 NX, NY, NZ, NC = 4, 4, 8, 2
 N_ROW = 32
-BATCHES = ((1, 8), (8, 16), (16, 17), (17, 18), (18, 19), (19, 32))
+PEERS = N_ROW - 1
+BATCHES = (0, 12, 36, 48, 60, 72, 90, 124)
 
 
 def split(value):
@@ -33,8 +34,8 @@
 
 
 def kernel(
-    owner, factors, stem, phase, out,
-    recv, mixed, cosine, sine, own, raw0, raw1, slots, from_y, summed, from_z, full,
+    owner, factors_hbm, stem_hbm, phase_hbm, out,
+    factors, stem, phase, turned, recv, mixed, cosine, sine, own, raw0, raw1, slots, from_y, summed, from_z, full,
     high, low, send, land, a_send, a_land, b_send, b_land, local,
 ):
     row, col = lax.axis_index("row"), lax.axis_index("col")
@@ -58,6 +59,15 @@
         peer = ((z_lo + i % 4) % 4) * 8 + (row + i // 4) % 8
         return peer
 
+    loads = [
+        pltpu.make_async_copy(stem_hbm.at[0], stem.at[0], local.at[0]),
+        pltpu.make_async_copy(stem_hbm.at[1], stem.at[1], local.at[1]),
+        pltpu.make_async_copy(factors_hbm, factors, local.at[2]),
+        pltpu.make_async_copy(phase_hbm, phase, local.at[3]),
+    ]
+    for load in loads:
+        load.start()
+
     barrier = pltpu.get_barrier_semaphore()
 
     def greet(device):
@@ -75,6 +85,15 @@
     def _(i):
         greet(at_z((1 - z_hi) * 4 + i))
 
+    for part in range(2):
+        loads[part].wait()
+
+        @pl.loop(0, 8)
+        def _(a):
+            for i in range(2):
+                turned[part, i, pl.ds(a, 128, stride=8)] = stem[part, a, pl.ds(i * 128, 128)].T
+
+    loads[2].wait()
     dot = functools.partial(jnp.dot, precision=lax.Precision.HIGHEST, preferred_element_type=F32)
     own[0] = dot(factors[0, 0], factors[1, 0]) - dot(factors[0, 1], factors[1, 1])
     own[1] = dot(factors[0, 0], factors[1, 1]) + dot(factors[0, 1], factors[1, 0])
@@ -87,24 +106,23 @@
             device_id=device, device_id_type=MESH,
         ).start()
 
-    def stem_batch(first, last):
-        @pl.loop(first, last)
+    def stem_batch(index):
+        @pl.loop(BATCHES[index], BATCHES[index + 1])
         def _(i):
-            peer = row_peer(i)
+            peer, b = row_peer(1 + i % PEERS), i // PEERS
             pltpu.make_async_remote_copy(
-                src_ref=stem.at[:, pl.ds(peer * 4, 4)],
-                dst_ref=recv.at[:, :, pl.ds(row * 8, 8)],
-                send_sem=a_send, recv_sem=a_land,
+                src_ref=turned.at[:, :, pl.ds((peer * 4 + b) * 8, 8)],
+                dst_ref=recv.at[:, b, :, pl.ds(row * 8, 8)],
+                send_sem=a_send, recv_sem=a_land.at[b],
                 device_id=(peer, col), device_id_type=MESH,
             ).start()
 
     push(own.at[1 - core], raw0.at[core], 0, at_core(1 - core))
-    keep = pltpu.make_async_copy(
-        stem.at[:, pl.ds(row * 4, 4)], recv.at[:, :, pl.ds(row * 8, 8)], local.at[0]
-    )
-    keep.start()
-    stem_batch(*BATCHES[0])
+    stem_batch(0)
     raw0[core] = own[core]
+    for b in range(4):
+        recv[:, b, :, pl.ds(row * 8, 8)] = turned[:, :, pl.ds((row * 4 + b) * 8, 8)]
+
     drained(raw0.at[0], land.at[0])
 
     @pl.loop(1, NX)
@@ -112,8 +130,9 @@
         peer = (x + i) % NX
         push(raw0.at[:, pl.ds(peer * 64, 64)], raw1.at[x], 1, at_x(peer))
 
-    stem_batch(*BATCHES[1])
+    stem_batch(1)
     raw1[x] = raw0[:, pl.ds(x * 64, 64)]
+    loads[3].wait()
 
     @pl.loop(0, STEPS)
     def _(step):
@@ -137,7 +156,7 @@
         peer = (y + i) % NY
         push(slots.at[:, pl.ds(peer * 16, 16)], from_y.at[y], 2, at_y(peer))
 
-    stem_batch(*BATCHES[2])
+    stem_batch(2)
     from_y[y] = slots[:, pl.ds(y * 16, 16)]
     drained(from_y.at[pl.ds(0, NY - 1)], land.at[2])
     total = (from_y[0] + from_y[1]) + (from_y[2] + from_y[3])
@@ -148,7 +167,7 @@
         peer = (z + i) % NZ
         push(summed.at[peer], from_z.at[z], 3, at_z(peer))
 
-    stem_batch(*BATCHES[3])
+    stem_batch(3)
     from_z[z] = summed[z]
     drained(from_z.at[pl.ds(0, NZ - 1)], land.at[3])
     total = from_z[0]
@@ -162,13 +181,14 @@
     def _(i):
         push(eighth, eighth, 4, at_z((z + i) % NZ))
 
-    stem_batch(*BATCHES[4])
+    stem_batch(4)
     drained(from_z.at[pl.ds(0, NZ - 1)], land.at[4])
 
     @pl.loop(1, NY)
     def _(i):
         push(mine, mine, 5, at_y((y + i) % NY))
 
+    stem_batch(5)
     drained(from_y.at[pl.ds(0, NY - 1)], land.at[5])
     quarter = full.at[:, core, x]
 
@@ -176,7 +196,7 @@
     def _(i):
         push(quarter, quarter, 6, at_x((x + i) % NX))
 
-    stem_batch(*BATCHES[5])
+    stem_batch(6)
     drained(full.at[pl.ds(0, NX - 1), 0], land.at[6])
     half = full.at[:, core]
     push(half, half, 7, at_core(1 - core))
@@ -189,12 +209,12 @@
                 branch = branch.T
             high[step, part], low[step, part] = split(branch)
 
-    keep.wait()
-    drained(stem.at[:, pl.ds(0, (N_ROW - 1) * 4)], a_land)
 
     @pl.loop(0, 4)
     def _(b):
-        real, imag = recv[0, b], recv[1, b]
+        drained(turned.at[:, :, pl.ds(0, PEERS * 8)], a_land.at[b])
+        real = jnp.concatenate([recv[0, b, 0], recv[0, b, 1]], axis=1)
+        imag = jnp.concatenate([recv[1, b, 0], recv[1, b, 1]], axis=1)
         for step in range(STEPS):
             xr, xi = split(real), split(imag)
             br = (high[step, 0], low[step, 0])
@@ -210,7 +230,7 @@
         mixed[b, 0] = real
         mixed[b, 1] = imag
         pltpu.make_async_copy(
-            mixed.at[b, :, pl.ds(row * 8, 8)], out.at[:, row * 4 + b], local.at[1]
+            mixed.at[b, :, pl.ds(row * 8, 8)], out.at[:, row * 4 + b], local.at[4]
         ).start()
 
         @pl.loop(1, N_ROW)
@@ -223,8 +243,8 @@
                 device_id=(peer, col), device_id_type=MESH,
             ).start()
 
-    drained(out.at[:, pl.ds(0, 4)], local.at[1])
-    drained(out.at[:, pl.ds(0, (N_ROW - 1) * 4)], b_land)
+    drained(out.at[:, pl.ds(0, 4)], local.at[4])
+    drained(out.at[:, pl.ds(0, PEERS * 4)], b_land)
     drained(raw0.at[0], send.at[0])
     drained(raw1.at[pl.ds(0, NX - 1)], send.at[1])
     drained(from_y.at[pl.ds(0, NY - 1)], send.at[2])
@@ -233,25 +253,28 @@
     drained(from_y.at[pl.ds(0, NY - 1)], send.at[5])
     drained(full.at[pl.ds(0, NX - 1), 0], send.at[6])
     drained(full.at[:, 0], send.at[7])
-    drained(stem.at[:, pl.ds(0, (N_ROW - 1) * 4)], a_send)
-    drained(out.at[:, pl.ds(0, (N_ROW - 1) * 4)], b_send)
+    drained(turned.at[:, :, pl.ds(0, PEERS * 32)], a_send)
+    drained(out.at[:, pl.ds(0, PEERS * 4)], b_send)
 
 
 def on_device(stem_slab, factors, branch_owner, entangle_phase):
-    stem = stem_slab.transpose(0, 3, 1, 2)
     vmem, dma = pltpu.VMEM, pltpu.SemaphoreType.DMA
     out = pl.pallas_call(
         kernel,
         out_shape=jax.ShapeDtypeStruct((2, 128, 8, 256), F32),
         in_specs=[
             pl.BlockSpec(memory_space=pltpu.SMEM),
-            pl.BlockSpec(memory_space=pltpu.VMEM),
             pl.BlockSpec(memory_space=pl.ANY),
-            pl.BlockSpec(memory_space=pltpu.VMEM),
+            pl.BlockSpec(memory_space=pl.ANY),
+            pl.BlockSpec(memory_space=pl.ANY),
         ],
         out_specs=pl.BlockSpec(memory_space=pl.ANY),
         scratch_shapes=[
-            vmem((2, 4, 256, 256), F32),
+            vmem((2, 2, 256, 256), F32),
+            vmem((2, 8, 256, 128), F32),
+            vmem((4, 256, 256), F32),
+            vmem((2, 2, 1024, 128), F32),
+            vmem((2, 4, 2, 256, 128), F32),
             vmem((4, 2, 256, 256), F32),
             vmem((4, 256, 256), F32),
             vmem((4, 256, 256), F32),
@@ -266,11 +289,11 @@
             vmem((4, 2, 256, 256), BF16),
             vmem((4, 2, 256, 256), BF16),
             dma((8,)), dma((8,)),
-            dma(()), dma(()), dma(()), dma(()),
-            dma((2,)),
+            dma(()), dma((4,)), dma(()), dma(()),
+            dma((5,)),
         ],
         compiler_params=pltpu.CompilerParams(collective_id=0, has_side_effects=True),
-    )(branch_owner, factors[0], stem, entangle_phase)
+    )(branch_owner, factors[0], stem_slab, entangle_phase)
     return out.transpose(0, 2, 3, 1)
 
 

time: 123 us -> 111 us (0.902)
  Pallas kernels: 117 us -> 108 us
  local copies, waits for them, and re-layouts: 5.97 us -> 2.94 us
    pallas_call x1, Pallas kernels: 117 us -> 108 us  [on_device(): pl.pallas_call(kernel, out_shape=jax.ShapeDtypeStruct((2, 128, 8, 256), F...]
    unnamed x1 -> x0, local copies, waits for them, and re-layouts: 3.03 us -> none
where the time goes in v2:
time: 111 us
  Pallas kernels  108 us (97%)
  local copies, waits for them, and re-layouts  2.94 us (3%)
    pallas_call x1, Pallas kernels, on_device(): pl.pallas_call(kernel, out_shape=jax.ShapeDtypeStruct((2, 128, 8, 256), F...  108 us
    transpose x1, local copies, waits for them, and re-layouts, on_device(): return out.transpose(0, 2, 3, 1)  2.94 us

profile of v2, /device:TPU:1, one launch (start us, length us, event | category | flops | bytes accessed | tf_op | source)
XLA Modules:
  0.0 110.9 jit_solution(4932375040407134977)
XLA Ops:
  0.0 108.0 %shard_map.46 = f32[2,128,8,256]{3,2,1,0:T(8,128)} custom-call(s32[4]{0:T(128)} %owner.1, f32[2,2,256,256]{3,2,1,0:T(8,128)} %bitcast.3, f32[2,8,256,128]{3,2,1,0:T(8,128)} %stem_hbm.1, f32[4,256,256]{2,1,0:T(8,128)} %phase_hbm.1), custom_call_target="tpu_custom_call" | custom-call | tf_op jit(solution)/shard_map/pallas_call | solution.py:262
  108.0 2.9 %copy.5 = f32[2,8,256,128]{3,2,1,0:T(8,128)} copy(f32[2,8,256,128]{2,1,3,0:T(8,128)} %bitcast.2) | data formatting | bytes 4194304 | tf_op jit(solution)/shard_map/transpose | solution.py:297

commit v3 on v2

--- a/solution.py
+++ b/solution.py
@@ -15,6 +15,7 @@
 NX, NY, NZ, NC = 4, 4, 8, 2
 N_ROW = 32
 PEERS = N_ROW - 1
+EARLY = 1
 BATCHES = (0, 12, 36, 48, 60, 72, 90, 124)
 
 
@@ -36,7 +37,7 @@
 def kernel(
     owner, factors_hbm, stem_hbm, phase_hbm, out,
     factors, stem, phase, turned, recv, mixed, cosine, sine, own, raw0, raw1, slots, from_y, summed, from_z, full,
-    high, low, send, land, a_send, a_land, b_send, b_land, local,
+    high, low, send, land, a_send, a_land, b_send, b_land, x_land, c_land, local,
 ):
     row, col = lax.axis_index("row"), lax.axis_index("col")
     core, y, z_lo = row % 2, (row // 2) % 4, row // 8
@@ -190,45 +191,45 @@
 
     stem_batch(5)
     drained(from_y.at[pl.ds(0, NY - 1)], land.at[5])
-    quarter = full.at[:, core, x]
-
-    @pl.loop(1, NX)
-    def _(i):
-        push(quarter, quarter, 6, at_x((x + i) % NX))
+
+    def pushed(part, sent, landed, device):
+        pltpu.make_async_remote_copy(
+            src_ref=part, dst_ref=part, send_sem=sent, recv_sem=landed,
+            device_id=device, device_id_type=MESH,
+        ).start()
+
+    for step in range(STEPS):
+        @pl.loop(1, NX)
+        def _(i):
+            pushed(full.at[step, core, x], send.at[6], x_land.at[step], at_x((x + i) % NX))
 
     stem_batch(6)
-    drained(full.at[pl.ds(0, NX - 1), 0], land.at[6])
-    half = full.at[:, core]
-    push(half, half, 7, at_core(1 - core))
-    drained(half, land.at[7])
-
-    for step in range(STEPS):
+
+    def arrived(b):
+        drained(turned.at[:, :, pl.ds(0, PEERS * 8)], a_land.at[b])
+        return tuple(jnp.concatenate([recv[c, b, 0], recv[c, b, 1]], axis=1) for c in range(2))
+
+    def prepare(step):
+        drained(full.at[step, 1 - core], c_land.at[step])
         for part in range(2):
             branch = full[step, part].reshape(256, 256)
             if step % 2:
                 branch = branch.T
             high[step, part], low[step, part] = split(branch)
 
-
-    @pl.loop(0, 4)
-    def _(b):
-        drained(turned.at[:, :, pl.ds(0, PEERS * 8)], a_land.at[b])
-        real = jnp.concatenate([recv[0, b, 0], recv[0, b, 1]], axis=1)
-        imag = jnp.concatenate([recv[1, b, 0], recv[1, b, 1]], axis=1)
-        for step in range(STEPS):
-            xr, xi = split(real), split(imag)
-            br = (high[step, 0], low[step, 0])
-            bi = (high[step, 1], low[step, 1])
-            if step % 2:
-                yr = dot3(br, xr) - dot3(bi, xi)
-                yi = dot3(bi, xr) + dot3(br, xi)
-            else:
-                yr = dot3(xr, br) - dot3(xi, bi)
-                yi = dot3(xr, bi) + dot3(xi, br)
-            real = yr * cosine[step] - yi * sine[step]
-            imag = yr * sine[step] + yi * cosine[step]
-        mixed[b, 0] = real
-        mixed[b, 1] = imag
+    def advance(step, real, imag):
+        xr, xi = split(real), split(imag)
+        br = (high[step, 0], low[step, 0])
+        bi = (high[step, 1], low[step, 1])
+        if step % 2:
+            yr = dot3(br, xr) - dot3(bi, xi)
+            yi = dot3(bi, xr) + dot3(br, xi)
+        else:
+            yr = dot3(xr, br) - dot3(xi, bi)
+            yi = dot3(xr, bi) + dot3(xi, br)
+        return yr * cosine[step] - yi * sine[step], yr * sine[step] + yi * cosine[step]
+
+    def send_off(b):
         pltpu.make_async_copy(
             mixed.at[b, :, pl.ds(row * 8, 8)], out.at[:, row * 4 + b], local.at[4]
         ).start()
@@ -242,6 +243,34 @@
                 send_sem=b_send, recv_sem=b_land,
                 device_id=(peer, col), device_id_type=MESH,
             ).start()
+
+    def early(step):
+        prepare(step)
+
+        @pl.loop(0, EARLY)
+        def _(b):
+            if step == 0:
+                real, imag = arrived(b)
+            else:
+                real, imag = mixed[b, 0], mixed[b, 1]
+            mixed[b, 0], mixed[b, 1] = advance(step, real, imag)
+            if step == STEPS - 1:
+                send_off(b)
+
+    for step in range(STEPS):
+        drained(full.at[0, 0, pl.ds(0, NX - 1)], x_land.at[step])
+        pushed(full.at[step, core], send.at[7], c_land.at[step], at_core(1 - core))
+        if step:
+            early(step - 1)
+    early(STEPS - 1)
+
+    @pl.loop(EARLY, 4)
+    def _(b):
+        real, imag = arrived(b)
+        for step in range(STEPS):
+            real, imag = advance(step, real, imag)
+        mixed[b, 0], mixed[b, 1] = real, imag
+        send_off(b)
 
     drained(out.at[:, pl.ds(0, 4)], local.at[4])
     drained(out.at[:, pl.ds(0, PEERS * 4)], b_land)
@@ -289,7 +318,7 @@
             vmem((4, 2, 256, 256), BF16),
             vmem((4, 2, 256, 256), BF16),
             dma((8,)), dma((8,)),
-            dma(()), dma((4,)), dma(()), dma(()),
+            dma(()), dma((4,)), dma(()), dma(()), dma((4,)), dma((4,)),
             dma((5,)),
         ],
         compiler_params=pltpu.CompilerParams(collective_id=0, has_side_effects=True),

time: 111 us -> 109 us (0.982)
  Pallas kernels: 108 us -> 106 us
    pallas_call x1, Pallas kernels: 108 us -> 106 us  [on_device(): pl.pallas_call(kernel, out_shape=jax.ShapeDtypeStruct((2, 128, 8, 256), F...]
where the time goes in v3:
time: 109 us
  Pallas kernels  106 us (97%)
  local copies, waits for them, and re-layouts  2.94 us (3%)
    pallas_call x1, Pallas kernels, on_device(): pl.pallas_call(kernel, out_shape=jax.ShapeDtypeStruct((2, 128, 8, 256), F...  106 us
    transpose x1, local copies, waits for them, and re-layouts, on_device(): return out.transpose(0, 2, 3, 1)  2.94 us

profile of v3, /device:TPU:1, one launch (start us, length us, event | category | flops | bytes accessed | tf_op | source)
XLA Modules:
  0.0 108.8 jit_solution(1284977811708499756)
XLA Ops:
  0.0 105.8 %shard_map.46 = f32[2,128,8,256]{3,2,1,0:T(8,128)} custom-call(s32[4]{0:T(128)} %owner.1, f32[2,2,256,256]{3,2,1,0:T(8,128)} %bitcast.3, f32[2,8,256,128]{3,2,1,0:T(8,128)} %stem_hbm.1, f32[4,256,256]{2,1,0:T(8,128)} %phase_hbm.1), custom_call_target="tpu_custom_call" | custom-call | tf_op jit(solution)/shard_map/pallas_call | solution.py:291
  105.9 2.9 %copy.5 = f32[2,8,256,128]{3,2,1,0:T(8,128)} copy(f32[2,8,256,128]{2,1,3,0:T(8,128)} %bitcast.2) | data formatting | bytes 4194304 | tf_op jit(solution)/shard_map/transpose | solution.py:326

commit v4 on v3

--- a/solution.py
+++ b/solution.py
@@ -37,7 +37,7 @@
 def kernel(
     owner, factors_hbm, stem_hbm, phase_hbm, out,
     factors, stem, phase, turned, recv, mixed, cosine, sine, own, raw0, raw1, slots, from_y, summed, from_z, full,
-    high, low, send, land, a_send, a_land, b_send, b_land, x_land, c_land, local,
+    high, low, send, land, a_send, a_land, b_send, b_land, x_land, c_land, local, crossed, told,
 ):
     row, col = lax.axis_index("row"), lax.axis_index("col")
     core, y, z_lo = row % 2, (row // 2) % 4, row // 8
@@ -82,9 +82,11 @@
     def _(i):
         greet(at_x((x + i) % NX))
 
-    @pl.loop(0, NZ // 2)
-    def _(i):
-        greet(at_z((1 - z_hi) * 4 + i))
+    middle = z_hi * 4 + z_lo == 3 + z_hi
+
+    @pl.when(middle)
+    def _():
+        greet(at_z(4 - z_hi))
 
     for part in range(2):
         loads[part].wait()
@@ -99,11 +101,24 @@
     own[0] = dot(factors[0, 0], factors[1, 0]) - dot(factors[0, 1], factors[1, 1])
     own[1] = dot(factors[0, 0], factors[1, 1]) + dot(factors[0, 1], factors[1, 0])
 
-    pl.semaphore_wait(barrier, N_ROW - 1 + NX - 1 + NZ // 2)
+    @pl.when(middle)
+    def _():
+        pl.semaphore_wait(barrier, N_ROW - 1 + NX - 1 + 1)
+        pl.semaphore_signal(crossed, inc=1, device_id=at_z(4 - z_hi), device_id_type=MESH)
+
+    @pl.when(jnp.logical_not(middle))
+    def _():
+        pl.semaphore_wait(barrier, N_ROW - 1 + NX - 1)
 
     def push(src, dst, stage, device):
         pltpu.make_async_remote_copy(
             src_ref=src, dst_ref=dst, send_sem=send.at[stage], recv_sem=land.at[stage],
+            device_id=device, device_id_type=MESH,
+        ).start()
+
+    def pushed(part, sent, landed, device):
+        pltpu.make_async_remote_copy(
+            src_ref=part, dst_ref=part, send_sem=sent, recv_sem=landed,
             device_id=device, device_id_type=MESH,
         ).start()
 
@@ -144,6 +159,15 @@
             sine[step, pl.ds(i * 8, 8)] = jnp.sin(angle)
 
     drained(raw1.at[pl.ds(0, NX - 1)], land.at[1])
+
+    @pl.when(middle)
+    def _():
+        pl.semaphore_wait(crossed, 1)
+
+        @pl.loop(1, NZ // 2)
+        def _(i):
+            pl.semaphore_signal(told, inc=1, device_id=at_z(z_hi * 4 + (z_lo + i) % 4), device_id_type=MESH)
+
     for step in range(STEPS):
         at = owner[step]
         at_row, at_col = lax.shift_right_logical(at, 3), at & 7
@@ -162,6 +186,10 @@
     drained(from_y.at[pl.ds(0, NY - 1)], land.at[2])
     total = (from_y[0] + from_y[1]) + (from_y[2] + from_y[3])
     summed[...] = total.reshape(NZ, 8, 256)
+
+    @pl.when(jnp.logical_not(middle))
+    def _():
+        pl.semaphore_wait(told, 1)
 
     @pl.loop(1, NZ)
     def _(i):
@@ -189,19 +217,19 @@
     def _(i):
         push(mine, mine, 5, at_y((y + i) % NY))
 
+    for step in range(STEPS):
+        @pl.loop(1, NX)
+        def _(i):
+            pushed(full.at[step, core, x, y], send.at[6], x_land.at[step], at_x((x + i) % NX))
+
     stem_batch(5)
     drained(from_y.at[pl.ds(0, NY - 1)], land.at[5])
 
-    def pushed(part, sent, landed, device):
-        pltpu.make_async_remote_copy(
-            src_ref=part, dst_ref=part, send_sem=sent, recv_sem=landed,
-            device_id=device, device_id_type=MESH,
-        ).start()
-
     for step in range(STEPS):
         @pl.loop(1, NX)
         def _(i):
-            pushed(full.at[step, core, x], send.at[6], x_land.at[step], at_x((x + i) % NX))
+            for j in range(1, NY):
+                pushed(full.at[step, core, x, (y + j) % NY], send.at[6], x_land.at[step], at_x((x + i) % NX))
 
     stem_batch(6)
 
@@ -320,6 +348,7 @@
             dma((8,)), dma((8,)),
             dma(()), dma((4,)), dma(()), dma(()), dma((4,)), dma((4,)),
             dma((5,)),
+            pltpu.SemaphoreType.REGULAR, pltpu.SemaphoreType.REGULAR,
         ],
         compiler_params=pltpu.CompilerParams(collective_id=0, has_side_effects=True),
     )(branch_owner, factors[0], stem_slab, entangle_phase)

time: 109 us -> 108 us (level)
  no operation moved by 1% of the time
where the time goes in v4:
time: 108 us
  Pallas kernels  105 us (97%)
  local copies, waits for them, and re-layouts  2.94 us (3%)
    pallas_call x1, Pallas kernels, on_device(): pl.pallas_call(kernel, out_shape=jax.ShapeDtypeStruct((2, 128, 8, 256), F...  105 us
    transpose x1, local copies, waits for them, and re-layouts, on_device(): return out.transpose(0, 2, 3, 1)  2.94 us

profile of v4, /device:TPU:1, one launch (start us, length us, event | category | flops | bytes accessed | tf_op | source)
XLA Modules:
  0.0 108.3 jit_solution(6840461982543818627)
XLA Ops:
  0.0 105.4 %shard_map.46 = f32[2,128,8,256]{3,2,1,0:T(8,128)} custom-call(s32[4]{0:T(128)} %owner.1, f32[2,2,256,256]{3,2,1,0:T(8,128)} %bitcast.3, f32[2,8,256,128]{3,2,1,0:T(8,128)} %stem_hbm.1, f32[4,256,256]{2,1,0:T(8,128)} %phase_hbm.1), custom_call_target="tpu_custom_call" | custom-call | tf_op jit(solution)/shard_map/pallas_call | solution.py:319
  105.4 2.9 %copy.5 = f32[2,8,256,128]{3,2,1,0:T(8,128)} copy(f32[2,8,256,128]{2,1,3,0:T(8,128)} %bitcast.2) | data formatting | bytes 4194304 | tf_op jit(solution)/shard_map/transpose | solution.py:355
